TPU v7x, 32 devices: a whole 2x2x4 slice. The times are simulated.
32 devices in a mesh: dp: 4 (over y, core), expert: 8 (over z, x).
Axes of the slice: x: 2, y: 2, z: 4, core: 2. Of those that a mesh axis runs over, the one named last changes fastest.
Arguments:
- hidden_in: bfloat16 [2048, 2048], P(('dp', 'expert')), may hold values from -6 to 6
- context: bfloat16 [2048, 2048], P(('dp', 'expert')), may hold values from -6 to 6
- out_proj: bfloat16 [2048, 2048], P(('dp', 'expert')), may hold values from -0.125 to 0.125
- norm_gain: float32 [2048], replicated, may hold values from 0.5 to 1.5
- router: bfloat16 [2048, 64], P(('dp', 'expert')), may hold values from -0.25 to 0.25
- expert_ids: int32 [2048, 8], P(('dp', 'expert')), may hold values from 0 to 63, as said below
- replica_expert: int32 [128], replicated, may hold values from 0 to 63, as said below
- split_pick: int32 [2048, 8], P(('dp', 'expert')), may hold values from 0 to 65535
- up_gate: bfloat16 [128, 2048, 2048], P(('dp', 'expert')), may hold values from -0.125 to 0.125
- down: bfloat16 [128, 1024, 2048], P(('dp', 'expert')), may hold values from -0.1875 to 0.1875
Outputs:
- layer_out: bfloat16 [2048, 2048], P(('dp', 'expert'))
Inputs may be any that keep to these rules, and one draw needn't show every extreme that they name: `expert_ids`: each row names 8 different experts. `replica_expert`: every expert is served by one replica or more.
All inputs are finite; a program needn't handle non-finite values.
Results may differ from a plain program's by a relative error of at most 0.004.
Values may be sent and summed in bfloat16 or wider, within the bound.
A program may use at most 128 MiB of HBM per device.

v0:
```python
import jax
import jax.numpy as jnp
from jax import lax
from jax.sharding import PartitionSpec as P


def rms_norm(residual, norm_gain):
    scale_back = lax.rsqrt(jnp.mean(residual * residual, axis=-1, keepdims=True) + 1e-05)
    return (residual * scale_back * norm_gain).astype(jnp.bfloat16)


def route_block(expert_ids, split_pick, replica_expert):
    replica_total = replica_expert.shape[0]
    replica_iota = lax.iota(jnp.int32, replica_total)
    same_expert = replica_expert[:, None] == replica_expert[None, :]
    earlier = replica_iota[:, None] > replica_iota[None, :]
    replica_rank = jnp.sum((same_expert & earlier).astype(jnp.int32), axis=1)
    serves = expert_ids[:, :, None] == replica_expert[None, None, :]
    replica_count = jnp.sum(serves.astype(jnp.int32), axis=-1)
    wanted = split_pick % replica_count
    matches = serves & (replica_rank[None, None, :] == wanted[:, :, None])
    replica = jnp.sum(jnp.where(matches, replica_iota[None, None, :], 0), axis=-1)
    flat_replica = replica.reshape(-1)
    pair_iota = lax.iota(jnp.int32, flat_replica.shape[0])
    same_target = flat_replica[:, None] == flat_replica[None, :]
    before = pair_iota[:, None] > pair_iota[None, :]
    slot_index = jnp.sum((same_target & before).astype(jnp.int32), axis=1)
    return (replica, slot_index.reshape(replica.shape))


def apply_experts(incoming, up_gate, down, capacity):
    arrived_shape = incoming.shape
    local_reps = up_gate.shape[0]
    hidden_units = down.shape[1]
    stacked = incoming.reshape(-1, local_reps, capacity, incoming.shape[-1])
    gate_up = jnp.einsum("sjcd,jdf->sjcf", stacked, up_gate, preferred_element_type=jnp.float32)
    hidden_act = (jax.nn.silu(gate_up[..., :hidden_units]) * gate_up[..., hidden_units:]).astype(
        jnp.bfloat16
    )
    expert_out = jnp.einsum("sjcf,jfd->sjcd", hidden_act, down, preferred_element_type=jnp.float32)
    return expert_out.astype(jnp.bfloat16).reshape(arrived_shape)


def per_device(
    hidden_in,
    context,
    out_proj,
    norm_gain,
    router,
    expert_ids,
    replica_expert,
    split_pick,
    up_gate,
    down,
):
    tok_rows, model_width = hidden_in.shape
    top_count = expert_ids.shape[1]
    replica_total = replica_expert.shape[0]
    local_reps = up_gate.shape[0]
    data_groups = lax.axis_size("dp")
    expert_groups = lax.axis_size("expert")
    capacity = max(2, 2 * tok_rows * top_count // replica_total)
    summed = jnp.dot(
        context,
        lax.all_gather(out_proj, ("dp", "expert"), axis=0, tiled=True),
        preferred_element_type=jnp.float32,
    )
    router_rows = lax.all_gather(router, ("dp", "expert"), axis=0, tiled=True)
    residual = hidden_in.astype(jnp.float32) + summed
    normed = rms_norm(residual, norm_gain)
    logits = jnp.dot(normed, router_rows, preferred_element_type=jnp.float32)
    hit_mask = expert_ids[:, :, None] == lax.iota(jnp.int32, logits.shape[1])[None, None, :]
    chosen = jnp.sum(jnp.where(hit_mask, logits[:, None, :], 0.0), axis=-1)
    raised = jnp.exp(chosen)
    route_weight = raised / jnp.sum(raised, axis=-1, keepdims=True)
    replica, slot_index = route_block(expert_ids, split_pick, replica_expert)
    within_cap = slot_index < capacity
    buffer_row = jnp.where(within_cap, replica * capacity + slot_index, -1).reshape(-1)
    slot_total = replica_total * capacity
    matches = buffer_row[None, :] == lax.iota(jnp.int32, slot_total)[:, None]
    filled = jnp.any(matches, axis=1)
    row_of_pair = lax.iota(jnp.int32, tok_rows * top_count) // top_count
    anchor = jnp.sum(jnp.where(matches, row_of_pair[None, :], 0), axis=1)
    outgoing = jnp.where(filled[:, None], normed[anchor], jnp.zeros((), jnp.bfloat16))
    outgoing = outgoing.reshape(data_groups, expert_groups, local_reps * capacity, model_width)
    incoming = lax.all_to_all(
        lax.all_to_all(outgoing, "expert", split_axis=1, concat_axis=1, tiled=True),
        "dp",
        split_axis=0,
        concat_axis=0,
        tiled=True,
    )
    results = apply_experts(incoming, up_gate, down, capacity)
    returned = lax.all_to_all(
        lax.all_to_all(results, "dp", split_axis=0, concat_axis=0, tiled=True),
        "expert",
        split_axis=1,
        concat_axis=1,
        tiled=True,
    )
    returned = returned.reshape(slot_total, model_width)
    safe_index = jnp.where(within_cap, replica * capacity + slot_index, 0)
    gathered = returned[safe_index]
    kept_weight = jnp.where(within_cap, route_weight, 0.0)
    layer_out = residual + jnp.sum(kept_weight[:, :, None] * gathered.astype(jnp.float32), axis=1)
    return layer_out.astype(jnp.bfloat16)


def per_device_gathered(
    hidden_in,
    context,
    out_proj,
    norm_gain,
    router,
    expert_ids,
    replica_expert,
    split_pick,
    up_gate,
    down,
):
    axes = ("dp", "expert")
    tok_rows, model_width = hidden_in.shape
    top_count = expert_ids.shape[1]
    replica_total = replica_expert.shape[0]
    local_reps = up_gate.shape[0]
    hidden_units = down.shape[1]
    blocks = lax.axis_size("dp") * lax.axis_size("expert")
    me = lax.axis_index("dp") * lax.axis_size("expert") + lax.axis_index("expert")
    capacity = max(2, 2 * tok_rows * top_count // replica_total)
    local_slots = local_reps * capacity
    proj_rows = lax.all_gather(out_proj, axes, axis=0, tiled=True)
    router_rows = lax.all_gather(router, axes, axis=0, tiled=True)
    replica, slot_index = route_block(expert_ids, split_pick, replica_expert)
    position = jnp.where(slot_index < capacity, replica * capacity + slot_index, -1)
    positions = lax.all_gather(position, axes, axis=0, tiled=False)
    summed = jnp.dot(context, proj_rows, preferred_element_type=jnp.float32)
    residual = hidden_in.astype(jnp.float32) + summed
    normed = rms_norm(residual, norm_gain)
    all_normed = lax.all_gather(normed, axes, axis=0, tiled=False)
    logits = jnp.dot(normed, router_rows, preferred_element_type=jnp.float32)
    hit_mask = expert_ids[:, :, None] == lax.iota(jnp.int32, logits.shape[1])[None, None, :]
    chosen = jnp.sum(jnp.where(hit_mask, logits[:, None, :], 0.0), axis=-1)
    raised = jnp.exp(chosen)
    route_weight = raised / jnp.sum(raised, axis=-1, keepdims=True)
    weights = lax.all_gather(route_weight, axes, axis=0, tiled=False)
    local_iota = lax.iota(jnp.int32, local_slots)
    hits = (positions - me * local_slots)[:, :, :, None] == local_iota
    pick = jnp.any(hits, axis=2)
    slot_weight = jnp.sum(jnp.where(hits, weights[:, :, :, None], 0.0), axis=2)
    expert_in = jnp.einsum(
        "btjc,btd->jbcd",
        pick.astype(jnp.bfloat16).reshape(blocks, tok_rows, local_reps, capacity),
        all_normed,
        preferred_element_type=jnp.float32,
    ).astype(jnp.bfloat16)
    expert_in = expert_in.reshape(local_reps, blocks * capacity, model_width)
    gate_up = jnp.einsum("jsd,jdf->jsf", expert_in, up_gate, preferred_element_type=jnp.float32)
    hidden_act = (jax.nn.silu(gate_up[..., :hidden_units]) * gate_up[..., hidden_units:]).astype(
        jnp.bfloat16
    )
    expert_out = jnp.einsum("jsf,jfd->jsd", hidden_act, down, preferred_element_type=jnp.float32)
    expert_out = expert_out.astype(jnp.bfloat16).reshape(local_reps, blocks, capacity, model_width)
    upper = slot_weight.astype(jnp.bfloat16)
    lower = (slot_weight - upper.astype(jnp.float32)).astype(jnp.bfloat16)
    split = jnp.stack([upper, lower]).reshape(2, blocks, tok_rows, local_reps, capacity)
    twice = jnp.broadcast_to(expert_out[None], (2,) + expert_out.shape)
    partial = jnp.einsum(
        "hbtjc,hjbcd->btd", split, twice, preferred_element_type=jnp.float32
    ).astype(jnp.bfloat16)
    combined = lax.psum_scatter(partial, axes, scatter_dimension=0, tiled=False)
    return (residual + combined.astype(jnp.float32)).astype(jnp.bfloat16)


def solution(mesh):
    device_count = mesh.shape["dp"] * mesh.shape["expert"]
    plan = per_device_gathered if device_count <= 32 else per_device
    return jax.shard_map(
        plan,
        mesh=mesh,
        in_specs=(
            P(("dp", "expert"), None),
            P(("dp", "expert"), None),
            P(("dp", "expert"), None),
            P(),
            P(("dp", "expert"), None),
            P(("dp", "expert"), None),
            P(),
            P(("dp", "expert"), None),
            P(("dp", "expert"), None, None),
            P(("dp", "expert"), None, None),
        ),
        out_specs=P(("dp", "expert"), None),
        check_vma=False,
    )
```

profile of v0, /device:TPU:0, one launch (start us, length us, event | category | flops | bytes accessed | tf_op | source)
XLA Modules:
  0.0 541.7 jit_solution(15114210386043356406)
XLA Ops:
  6.5 0.0 copy-start
  6.5 0.0 all-gather.4.cloned.1.call-start
  6.5 0.7 all-gather.4.cloned.1.call-update
  7.3 0.0 copy-start.3
  7.3 0.0 copy-start.4
  7.3 0.0 copy-start.5
  7.3 0.0 copy-start.6
  7.3 0.0 copy-start.2
  7.3 0.0 all-gather.6.cloned.1.call-start
  7.4 83.1 %all-gather.4.cloned.1.call-done = bf16[2048,2048]{1,0:T(8,128)(2,1)} async-done(((bf16[64,2048]{1,0:T(8,128)(2,1)}), bf16[2048,2048]{1,0:T(8,128)(2,1)}) %all-gather.4.cloned.1.call-update) | async-done | bytes 8388624 | tf_op jit(solution)/shard_map/all_gather | solution.py:131
  90.5 0.0 copy-done
  90.5 5.1 multiply_reduce_fusion
  95.6 0.0 copy-done.3
  95.6 0.8 multiply_convert_fusion
  96.4 0.0 all-gather.6.cloned.1.call-update
  96.4 0.0 reduce-scatter.2.cloned.1.call-start
  96.5 0.0 copy-done.4
  96.5 0.1 copy.28
  96.6 0.0 copy-done.5
  96.6 0.1 copy.29
  96.7 0.2 convert_reduce_fusion.1
  96.9 1.2 fusion.15
  98.1 0.4 add_select_fusion
  98.5 1.3 select_reduce_fusion.2
  99.8 0.1 eq.94
  99.9 0.3 convert_reduce_fusion
  100.1 0.1 reshape.126
  100.3 0.1 copy.30
  100.3 68.0 %all_gather.21 = s32[32,64,8]{1,2,0:T(8,128)S(1)} all-gather(s32[1,64,8]{1,2,0:T(8,128)S(1)} %copy.30), channel_id=1, replica_groups=mesh['dp'=4,'expert'=8] {'dp','expert'}, dimensions={0}, use_global_device_ids=true | all-gather | bytes 67584 | tf_op jit(solution)/shard_map/all_gather | solution.py:135
  168.3 66.4 %all_gather.22 = bf16[2048,64]{1,0:T(8,128)(2,1)S(1)} all-gather(bf16[64,64]{1,0:T(8,128)(2,1)S(1)} %copy-done.2), channel_id=1, replica_groups=mesh['dp'=4,'expert'=8] {'dp','expert'}, dimensions={0}, use_global_device_ids=true | all-gather | bytes 270336 | tf_op jit(solution)/shard_map/all_gather | solution.py:132
  234.7 0.7 fusion.5
  235.3 1.2 fusion.20
  236.5 0.2 select_reduce_fusion.1
  236.7 0.1 exponential_reduce_fusion
  236.8 0.1 bitcast_divide_fusion
  236.9 0.1 copy.32
  237.0 66.4 %all_gather.23 = f32[32,64,8]{1,2,0:T(8,128)S(1)} all-gather(f32[1,64,8]{1,2,0:T(8,128)S(1)} %copy.32), channel_id=1, replica_groups=mesh['dp'=4,'expert'=8] {'dp','expert'}, dimensions={0}, use_global_device_ids=true | all-gather | bytes 67584 | tf_op jit(solution)/shard_map/all_gather | solution.py:145
  303.4 0.9 select_reduce_fusion
  304.3 0.1 fusion.14
  304.4 0.0 all-gather.6.cloned.1.call-done
  304.4 6.6 %fusion.6 = bf16[4,32,8,2048]{3,2,0,1:T(8,128)(2,1)} fusion(bf16[32,64,2048]{2,1,0:T(8,128)(2,1)} %bitcast.42, pred[32,64,32]{1,2,0:T(8,128)(4,1)S(1)} %fusion.5), kind=kOutput, calls=%fused_computation.12 | convolution fusion | flops 270532608 | bytes 12648448
  311.0 18.3 %fusion.1 = f32[4,256,2048]{2,1,0:T(8,128)} fusion(bf16[4,2048,2048]{2,1,0:T(8,128)(2,1)} %param.18, bf16[4,32,8,2048]{3,2,0,1:T(8,128)(2,1)} %fusion.6), kind=kOutput, calls=%fused_computation.4 | convolution fusion | flops 8589934592 | bytes 46137344 | tf_op jit(solution)/shard_map/jsd,jdf->jsf/dot_general | solution.py:157
  329.3 15.0 %convert_bitcast_fusion = bf16[4,32,8,2048]{3,2,1,0:T(8,128)(2,1)} fusion(bf16[4,1024,2048]{2,1,0:T(8,128)(2,1)} %param.19, f32[4,256,2048]{2,1,0:T(8,128)} %fusion.1), kind=kOutput, calls=%fused_computation.8 | convolution fusion | flops 4303355904 | bytes 29360128 | tf_op jit(solution)/shard_map/jsf,jfd->jsd/dot_general | solution.py:161
  344.3 6.6 %bitcast_convert_fusion = bf16[32,64,2048]{2,1,0:T(8,128)(2,1)} fusion(bf16[1,32,64,4,8]{2,4,3,1,0:T(8,128)(2,1)S(1)} %get-tuple-element.5, bf16[1,32,64,4,8]{2,4,3,1,0:T(8,128)(2,1)S(1)} %get-tuple-element.6, bf16[4,32,8,2048]{3,2,1,0:T(8,128)(2,1)} %convert_bitcast_fusion), kind=kOutput, calls=%fused_computation | convolution fusion | flops 541196288 | bytes 12845056 | tf_op jit(solution)/shard_map/hbtjc,hjbcd->btd/dot_general | solution.py:167
  350.8 0.0 reduce-scatter.2.cloned.1.call-update
  350.9 182.6 %reduce-scatter.2.cloned.1.call-done = bf16[1,64,2048]{2,1,0:T(8,128)(2,1)} async-done(((bf16[32,64,2048]{2,1,0:T(8,128)(2,1)}), bf16[1,64,2048]{2,1,0:T(8,128)(2,1)}) %reduce-scatter.2.cloned.1.call-update) | async-done | bytes 262160 | tf_op jit(solution)/shard_map/reduce_scatter | solution.py:170
  533.4 1.7 fusion.13
  535.1 0.0 copy-done.1
  (6 shorter events, 0.0 us)
Async XLA Ops:
  6.5 84.0 %copy-start = (bf16[64,2048]{1,0:T(8,128)(2,1)S(1)}, bf16[64,2048]{1,0:T(8,128)(2,1)}, u32[]{:S(2)}) copy-start(bf16[64,2048]{1,0:T(8,128)(2,1)} %param.11) | copy-start | bytes 786436
  6.5 84.0 %all-gather.4.cloned.1.call-start = ((), (), s32[]{:S(2)}) async-start(), calls=%async_computation.1 | async-start | bytes 8650752 | tf_op jit(solution)/shard_map/all_gather | solution.py:131
  7.3 88.3 %copy-start.3 = (f32[2048]{0:T(1024)S(1)}, f32[2048]{0:T(1024)}, u32[]{:S(2)}) copy-start(f32[2048]{0:T(1024)} %param.13) | copy-start | bytes 24580
  7.3 89.2 %copy-start.4 = (s32[64,8]{0,1:T(8,128)S(1)}, s32[64,8]{0,1:T(8,128)}, u32[]{:S(2)}) copy-start(s32[64,8]{0,1:T(8,128)} %param.15) | copy-start | bytes 6148
  7.3 89.3 %copy-start.5 = (s32[64,8]{0,1:T(8,128)S(1)}, s32[64,8]{0,1:T(8,128)}, u32[]{:S(2)}) copy-start(s32[64,8]{0,1:T(8,128)} %param.17) | copy-start | bytes 6148
  7.3 89.4 %copy-start.6 = (s32[128]{0:T(128)S(1)}, s32[128]{0:T(128)}, u32[]{:S(2)}) copy-start(s32[128]{0:T(128)} %param.16) | copy-start | bytes 1540
  7.3 161.0 %copy-start.2 = (bf16[64,64]{1,0:T(8,128)(2,1)S(1)}, bf16[64,64]{1,0:T(8,128)(2,1)}, u32[]{:S(2)}) copy-start(bf16[64,64]{1,0:T(8,128)(2,1)} %param.14) | copy-start | bytes 24580
  7.3 297.1 %all-gather.6.cloned.1.call-start = ((), (), s32[]{:S(2)}) async-start(), calls=%async_computation.3 | async-start | bytes 8650752 | tf_op jit(solution)/shard_map/all_gather | solution.py:139
  96.4 437.0 %reduce-scatter.2.cloned.1.call-start = ((), (), s32[]{:S(2)}) async-start(), calls=%async_computation.2 | async-start | bytes 8650752 | tf_op jit(solution)/shard_map/reduce_scatter | solution.py:170
  350.8 184.3 %copy-start.1 = (bf16[64,2048]{1,0:T(8,128)(2,1)S(1)}, bf16[64,2048]{1,0:T(8,128)(2,1)}, u32[]{:S(2)}) copy-start(bf16[64,2048]{1,0:T(8,128)(2,1)} %param.11) | copy-start | bytes 786436
Sparse Core Ops, SparseCore 0:
  10.3 80.1 all-gather.3
  96.6 77.7 all-gather.5
  351.0 182.3 reduce-scatter.1
where the time goes:
time: 542 us
  waiting for transfers between devices  266 us (49%)
  blocking collectives  201 us (37%)
  matrix products  52.6 us (10%)
  between operations  13.3 us (2%)
  other arithmetic  7.94 us (1%)
    reduce_scatter x1, waiting for transfers between devices, per_device_gathered(): combined = lax.psum_scatter(partial, axes, scatter_dimension=0, tiled=False)  183 us
    all_gather x1, waiting for transfers between devices, per_device_gathered(): proj_rows = lax.all_gather(out_proj, axes, axis=0, tiled=True)  83.1 us
    all_gather x1, blocking collectives, per_device_gathered(): positions = lax.all_gather(position, axes, axis=0, tiled=False)  68 us
    all_gather x1, blocking collectives, per_device_gathered(): weights = lax.all_gather(route_weight, axes, axis=0, tiled=False)  66.4 us
    all_gather x1, blocking collectives, per_device_gathered(): router_rows = lax.all_gather(router, axes, axis=0, tiled=True)  66.4 us
    dot_general x1, matrix products, per_device_gathered(): jnp.einsum('jsd,jdf->jsf', expert_in, up_gate, preferred_element_type=jnp...  18.3 us
    dot_general x1, matrix products, per_device_gathered(): jnp.einsum('jsf,jfd->jsd', hidden_act, down, preferred_element_type=jnp.f...  15 us
  transfers between devices with their start and end apart: 3, of which 2 were waited for; matrix products, arithmetic and copies ran while one was open for 1% of the time, Pallas kernels for 0%

commit v1 on v0

--- a/solution.py
+++ b/solution.py
@@ -128,8 +128,11 @@
     me = lax.axis_index("dp") * lax.axis_size("expert") + lax.axis_index("expert")
     capacity = max(2, 2 * tok_rows * top_count // replica_total)
     local_slots = local_reps * capacity
-    proj_rows = lax.all_gather(out_proj, axes, axis=0, tiled=True)
-    router_rows = lax.all_gather(router, axes, axis=0, tiled=True)
+    proj_rows, router_rows = jnp.split(
+        lax.all_gather(jnp.concatenate([out_proj, router], axis=1), axes, axis=0, tiled=True),
+        [out_proj.shape[1]],
+        axis=1,
+    )
     replica, slot_index = route_block(expert_ids, split_pick, replica_expert)
     position = jnp.where(slot_index < capacity, replica * capacity + slot_index, -1)
     positions = lax.all_gather(position, axes, axis=0, tiled=False)

time: 542 us -> 476 us (0.88)
  blocking collectives: 201 us -> 132 us
    all_gather x1 -> x0, blocking collectives: 66.4 us -> none  [per_device_gathered(): router_rows = lax.all_gather(router, axes, axis=0, tiled=True)]
  transfers between devices with their start and end apart: 3 -> 3, of which waited for: 2 -> 2; matrix products, arithmetic and copies ran while one was open for 1% -> 2% of each run, Pallas kernels for 0% -> 0%
where the time goes in v1:
time: 476 us
  waiting for transfers between devices  267 us (56%)
  blocking collectives  132 us (28%)
  matrix products  52.8 us (11%)
  between operations  13.3 us (3%)
  other arithmetic  9.69 us (2%)
    reduce_scatter x1, waiting for transfers between devices, per_device_gathered(): combined = lax.psum_scatter(partial, axes, scatter_dimension=0, tiled=False)  183 us
    all_gather x1, waiting for transfers between devices, per_device_gathered(): lax.all_gather(jnp.concatenate([out_proj, router], axis=1), axes, axis=0,...  84.3 us
    all_gather x1, blocking collectives, per_device_gathered(): positions = lax.all_gather(position, axes, axis=0, tiled=False)  67.9 us
    all_gather x1, blocking collectives, per_device_gathered(): weights = lax.all_gather(route_weight, axes, axis=0, tiled=False)  64.2 us
    dot_general x1, matrix products, per_device_gathered(): jnp.einsum('jsd,jdf->jsf', expert_in, up_gate, preferred_element_type=jnp...  18.3 us
    dot_general x1, matrix products, per_device_gathered(): jnp.einsum('jsf,jfd->jsd', hidden_act, down, preferred_element_type=jnp.f...  15 us
  transfers between devices with their start and end apart: 3, of which 2 were waited for; matrix products, arithmetic and copies ran while one was open for 2% of the time, Pallas kernels for 0%

profile of v1, /device:TPU:0, one launch (start us, length us, event | category | flops | bytes accessed | tf_op | source)
XLA Modules:
  0.0 475.9 jit_solution(11589045134433765110)
XLA Ops:
  6.5 0.0 copy-start
  6.5 0.0 all-gather.4.cloned.1.call-start
  6.5 1.8 pad_maximum_fusion
  8.3 0.0 all-gather.4.cloned.1.call-update
  8.3 0.0 copy-start.2
  8.3 0.0 copy-start.3
  8.3 0.0 copy-start.4
  8.4 0.0 copy-start.5
  8.4 0.0 all-gather.6.cloned.1.call-start
  8.4 84.3 %all-gather.4.cloned.1.call-done = bf16[2048,2112]{1,0:T(8,128)(2,1)} async-done(((bf16[64,2112]{1,0:T(8,128)(2,1)}), bf16[2048,2112]{1,0:T(8,128)(2,1)}) %all-gather.4.cloned.1.call-update) | async-done | bytes 8650768 | tf_op jit(solution)/shard_map/all_gather | solution.py:132
  92.8 0.0 copy-done
  92.8 5.1 %multiply_reduce_fusion = (f32[64]{0:T(128)S(1)}, f32[64,2048]{1,0:T(8,128)S(1)}) fusion(bf16[64,2048]{1,0:T(8,128)(2,1)S(1)} %copy-done, bf16[2048,2112]{1,0:T(8,128)(2,1)} %all-gather.4.cloned.1.call-done, bf16[64,2048]{1,0:T(8,128)(2,1)} %param.10), kind=kOutput, calls=%fused_computation.32 | convolution fusion | flops 537395136 | bytes 9437440 | tf_op jit(solution)/shard_map/dot_general | solution.py:139
  97.8 0.0 copy-done.2
  97.9 0.8 multiply_convert_fusion
  98.7 0.0 all-gather.6.cloned.1.call-update
  98.7 0.0 reduce-scatter.2.cloned.1.call-start
  98.8 0.0 copy-done.3
  98.8 0.1 copy.28
  98.9 0.0 copy-done.4
  98.9 0.1 copy.29
  98.9 0.0 copy-done.5
  98.9 0.2 convert_reduce_fusion.1
  99.1 1.2 fusion.25
  100.4 0.4 add_select_fusion
  100.7 1.3 select_reduce_fusion.2
  102.1 0.1 eq.94
  102.1 0.3 convert_reduce_fusion
  102.4 0.1 reshape.126
  102.5 0.1 copy.30
  102.6 67.9 %all_gather.18 = s32[32,64,8]{1,2,0:T(8,128)S(1)} all-gather(s32[1,64,8]{1,2,0:T(8,128)S(1)} %copy.30), channel_id=1, replica_groups=mesh['dp'=4,'expert'=8] {'dp','expert'}, dimensions={0}, use_global_device_ids=true | all-gather | bytes 67584 | tf_op jit(solution)/shard_map/all_gather | solution.py:138
  170.5 0.7 fusion.7
  171.2 1.3 fusion.18
  172.5 0.2 select_reduce_fusion.1
  172.8 0.1 exponential_reduce_fusion
  172.9 0.1 bitcast_divide_fusion
  173.0 0.1 copy.32
  173.0 64.2 %all_gather.19 = f32[32,64,8]{1,2,0:T(8,128)S(1)} all-gather(f32[1,64,8]{1,2,0:T(8,128)S(1)} %copy.32), channel_id=1, replica_groups=mesh['dp'=4,'expert'=8] {'dp','expert'}, dimensions={0}, use_global_device_ids=true | all-gather | bytes 67584 | tf_op jit(solution)/shard_map/all_gather | solution.py:148
  237.3 0.9 select_reduce_fusion
  238.1 0.1 fusion.24
  238.2 0.0 all-gather.6.cloned.1.call-done
  238.3 6.6 %fusion.8 = bf16[4,32,8,2048]{3,2,0,1:T(8,128)(2,1)} fusion(bf16[32,64,2048]{2,1,0:T(8,128)(2,1)} %bitcast.44, pred[32,64,32]{1,2,0:T(8,128)(4,1)S(1)} %fusion.7), kind=kOutput, calls=%fused_computation.14 | convolution fusion | flops 270532608 | bytes 12648448
  244.8 18.3 %fusion.3 = f32[4,256,2048]{2,1,0:T(8,128)} fusion(bf16[4,2048,2048]{2,1,0:T(8,128)(2,1)} %param.18, bf16[4,32,8,2048]{3,2,0,1:T(8,128)(2,1)} %fusion.8), kind=kOutput, calls=%fused_computation.6 | convolution fusion | flops 8589934592 | bytes 46137344 | tf_op jit(solution)/shard_map/jsd,jdf->jsf/dot_general | solution.py:160
  263.1 15.0 %convert_bitcast_fusion = bf16[4,32,8,2048]{3,2,1,0:T(8,128)(2,1)} fusion(bf16[4,1024,2048]{2,1,0:T(8,128)(2,1)} %param.19, f32[4,256,2048]{2,1,0:T(8,128)} %fusion.3), kind=kOutput, calls=%fused_computation.10 | convolution fusion | flops 4303355904 | bytes 29360128 | tf_op jit(solution)/shard_map/jsf,jfd->jsd/dot_general | solution.py:164
  278.1 6.6 %bitcast_convert_fusion = bf16[32,64,2048]{2,1,0:T(8,128)(2,1)} fusion(bf16[1,32,64,4,8]{2,4,3,1,0:T(8,128)(2,1)S(1)} %get-tuple-element.5, bf16[1,32,64,4,8]{2,4,3,1,0:T(8,128)(2,1)S(1)} %get-tuple-element.6, bf16[4,32,8,2048]{3,2,1,0:T(8,128)(2,1)} %convert_bitcast_fusion), kind=kOutput, calls=%fused_computation | convolution fusion | flops 541196288 | bytes 12845056 | tf_op jit(solution)/shard_map/hbtjc,hjbcd->btd/dot_general | solution.py:170
  284.6 0.0 reduce-scatter.2.cloned.1.call-update
  284.7 183.0 %reduce-scatter.2.cloned.1.call-done = bf16[1,64,2048]{2,1,0:T(8,128)(2,1)} async-done(((bf16[32,64,2048]{2,1,0:T(8,128)(2,1)}), bf16[1,64,2048]{2,1,0:T(8,128)(2,1)}) %reduce-scatter.2.cloned.1.call-update) | async-done | bytes 262160 | tf_op jit(solution)/shard_map/reduce_scatter | solution.py:173
  467.6 1.7 fusion.23
  469.3 0.0 copy-done.1
  (4 shorter events, 0.0 us)
Async XLA Ops:
  6.5 86.2 %copy-start = (bf16[64,2048]{1,0:T(8,128)(2,1)S(1)}, bf16[64,2048]{1,0:T(8,128)(2,1)}, u32[]{:S(2)}) copy-start(bf16[64,2048]{1,0:T(8,128)(2,1)} %param.11) | copy-start | bytes 786436
  6.5 86.2 %all-gather.4.cloned.1.call-start = ((), (), s32[]{:S(2)}) async-start(), calls=%async_computation.1 | async-start | bytes 9191424 | tf_op jit(solution)/shard_map/all_gather | solution.py:132
  8.3 89.5 %copy-start.2 = (f32[2048]{0:T(1024)S(1)}, f32[2048]{0:T(1024)}, u32[]{:S(2)}) copy-start(f32[2048]{0:T(1024)} %param.13) | copy-start | bytes 24580
  8.3 90.4 %copy-start.3 = (s32[64,8]{0,1:T(8,128)S(1)}, s32[64,8]{0,1:T(8,128)}, u32[]{:S(2)}) copy-start(s32[64,8]{0,1:T(8,128)} %param.15) | copy-start | bytes 6148
  8.3 90.5 %copy-start.4 = (s32[64,8]{0,1:T(8,128)S(1)}, s32[64,8]{0,1:T(8,128)}, u32[]{:S(2)}) copy-start(s32[64,8]{0,1:T(8,128)} %param.17) | copy-start | bytes 6148
  8.4 90.6 %copy-start.5 = (s32[128]{0:T(128)S(1)}, s32[128]{0:T(128)}, u32[]{:S(2)}) copy-start(s32[128]{0:T(128)} %param.16) | copy-start | bytes 1540
  8.4 229.9 %all-gather.6.cloned.1.call-start = ((), (), s32[]{:S(2)}) async-start(), calls=%async_computation.3 | async-start | bytes 8650752 | tf_op jit(solution)/shard_map/all_gather | solution.py:142
  98.7 368.9 %reduce-scatter.2.cloned.1.call-start = ((), (), s32[]{:S(2)}) async-start(), calls=%async_computation.2 | async-start | bytes 8650752 | tf_op jit(solution)/shard_map/reduce_scatter | solution.py:173
  284.6 184.7 %copy-start.1 = (bf16[64,2048]{1,0:T(8,128)(2,1)S(1)}, bf16[64,2048]{1,0:T(8,128)(2,1)}, u32[]{:S(2)}) copy-start(bf16[64,2048]{1,0:T(8,128)(2,1)} %param.11) | copy-start | bytes 786436
Sparse Core Ops, SparseCore 0:
  10.3 82.4 all-gather.3
  98.8 77.1 all-gather.5
  284.8 182.7 reduce-scatter.1
